TPU v7x, 32 devices: a whole 2x2x4 slice. The times are simulated.
32 devices in a mesh: grp: 8 (over z, x), seq: 4 (over y, core).
Axes of the slice: x: 2, y: 2, z: 4, core: 2. Of those that a mesh axis runs over, the one named last changes fastest.
Arguments:
- frames_in: bfloat16 [8192, 512], P(('grp', 'seq')), may hold values from -6 to 6
- norm_gain: float32 [512], replicated, may hold values from 0.25 to 1.75
- qkv_weight: bfloat16 [512, 1536], replicated, may hold values from -0.25 to 0.25
- conv_weight: float32 [4, 1536], replicated, may hold values from -3 to 3
- out_weight: bfloat16 [512, 512], replicated, may hold values from -0.25 to 0.25
- head_gain: float32 [512], replicated, may hold values from 0.25 to 1.75
- ffn_gain: float32 [512], replicated, may hold values from 0.25 to 1.75
- up_weight: bfloat16 [512, 2048], P(None, 'seq'), may hold values from -0.25 to 0.25
- down_weight: bfloat16 [2048, 512], P('seq'), may hold values from -0.125 to 0.125
Outputs:
- encoded: bfloat16 [8192, 512], P(('grp', 'seq'))
All inputs are finite; a program needn't handle non-finite values.
Results may differ from a plain program's by a relative error of at most 0.007.
Values may be sent and summed in bfloat16 or wider, within the bound.
No kernel may reach another device: no remote copies, remote signals or barrier semaphores. Data moves between devices by JAX's collectives and lax.ppermute only.
A program may use at most 256 MiB of HBM per device.

v0:
```python
import jax
import jax.numpy as jnp
from jax import lax
from jax.sharding import PartitionSpec as P

HEADS = 8
HEAD = 64
KERNEL = 4
BLOCK = 256


EPSILON = 1e-05


def from_behind(block, axis, distance):
    devices = range(lax.axis_size(axis))
    route = [(i - distance, i) for i in devices if i - distance in devices]
    return lax.ppermute(block, axis, route)


def prefix_2(x, axis, combine, identity):
    length, place = (lax.axis_size(axis), lax.axis_index(axis))
    everything = lax.all_gather(x, axis)
    start = jnp.broadcast_to(jnp.asarray(identity, x.dtype), x.shape)

    def turn(k, before):
        reached = k < place
        new = combine(before, everything[k])
        return jnp.where(reached, new, before)

    return lax.fori_loop(0, length, turn, start)


def rms_scale(values_in, gain):
    mean_square = jnp.mean(values_in * values_in, axis=-1, keepdims=True)
    return values_in * lax.rsqrt(mean_square + EPSILON) * gain


def add_states(earlier, later):
    return earlier + later


def attend_block(pieces):
    queries, key_rows, value_rows, state_low = pieces
    block_len = queries.shape[0]
    causal = jnp.arange(block_len)[:, None] >= jnp.arange(block_len)[None, :]
    scores = jnp.einsum("thd,shd->hts", queries, key_rows, preferred_element_type=jnp.float32)
    scores = jnp.where(causal[None], scores, 0.0).astype(jnp.bfloat16)
    local_part = jnp.einsum("hts,shd->thd", scores, value_rows, preferred_element_type=jnp.float32)
    carried_part = jnp.einsum(
        "thd,hde->the", queries, state_low, preferred_element_type=jnp.float32
    )
    return local_part + carried_part


def body(
    frames_in,
    norm_gain,
    qkv_weight,
    conv_weight,
    out_weight,
    head_gain,
    ffn_gain,
    up_weight,
    down_weight,
):
    row_count, model_width = frames_in.shape
    block_count = row_count // BLOCK
    lag_rows = KERNEL - 1
    normed = rms_scale(frames_in.astype(jnp.float32), norm_gain).astype(jnp.bfloat16)
    projected = jnp.dot(normed, qkv_weight, preferred_element_type=jnp.float32).astype(jnp.bfloat16)
    before = from_behind(projected[row_count - lag_rows :], ("grp", "seq"), 1)
    extended = jnp.concatenate([before, projected], axis=0).astype(jnp.float32)
    convolved = jnp.zeros((row_count, 3 * model_width), jnp.float32)
    for offset in range(KERNEL):
        convolved = (
            convolved
            + conv_weight[offset] * extended[lag_rows - offset : lag_rows - offset + row_count]
        )
    block_shape = (block_count, BLOCK, HEADS, HEAD)
    queries = jax.nn.silu(convolved[:, :model_width]).astype(jnp.bfloat16).reshape(block_shape)
    key_rows = (
        jax.nn.silu(convolved[:, model_width : 2 * model_width])
        .astype(jnp.bfloat16)
        .reshape(block_shape)
    )
    value_rows = convolved[:, 2 * model_width :].astype(jnp.bfloat16).reshape(block_shape)
    block_states = jnp.einsum(
        "bshd,bshe->bhde", key_rows, value_rows, preferred_element_type=jnp.float32
    )
    device_state = jnp.sum(block_states, axis=0)
    zero_state = jnp.zeros_like(device_state)
    prefix = prefix_2(device_state, ("grp", "seq"), add_states, zero_state)
    earlier_blocks = jnp.concatenate(
        [zero_state[None], jnp.cumsum(block_states[:-1], axis=0)], axis=0
    )
    state_low = (prefix[None] + earlier_blocks).astype(jnp.bfloat16)
    attended = lax.map(attend_block, (queries, key_rows, value_rows, state_low))
    head_square = jnp.mean(attended * attended, axis=-1, keepdims=True)
    headed = (attended * lax.rsqrt(head_square + EPSILON)).reshape(
        row_count, model_width
    ) * head_gain
    headed = headed.astype(jnp.bfloat16)
    residual = frames_in.astype(jnp.float32) + jnp.dot(
        headed, out_weight, preferred_element_type=jnp.float32
    )
    normed_ffn = rms_scale(residual, ffn_gain).astype(jnp.bfloat16)
    inner_act = jax.nn.gelu(
        jnp.dot(
            normed_ffn,
            lax.all_gather(up_weight, "seq", axis=1, tiled=True),
            preferred_element_type=jnp.float32,
        )
    ).astype(jnp.bfloat16)
    ffn_out = jnp.dot(
        inner_act,
        lax.all_gather(down_weight, "seq", axis=0, tiled=True),
        preferred_element_type=jnp.float32,
    )
    return (residual + ffn_out).astype(jnp.bfloat16)


def solution(mesh):
    in_specs = (
        P(("grp", "seq"), None),
        P(),
        P(),
        P(),
        P(),
        P(),
        P(),
        P(None, "seq"),
        P("seq", None),
    )
    out_specs = P(("grp", "seq"), None)
    return jax.shard_map(body, mesh=mesh, in_specs=in_specs, out_specs=out_specs, check_vma=False)
```

profile of v0, /device:TPU:0, one launch (start us, length us, event | category | flops | bytes accessed | tf_op | source)
XLA Modules:
  0.0 155.0 jit_solution(5738290194023966455)
XLA Ops:
  6.5 1.2 fusion.21
  8.0 1.6 %convolution_convert_fusion = bf16[256,1536]{1,0:T(8,128)(2,1)S(1)} fusion(bf16[512,1536]{1,0:T(8,128)(2,1)S(1)} %copy-done, bf16[256,512]{1,0:T(8,128)(2,1)} %param.11, f32[512]{0:T(512)} %param.12, f32[256]{0:T(256)S(1)} %add_rsqrt_fusion.2), kind=kOutput, calls=%fused_computation.2 | convolution fusion | flops 403570688 | bytes 2624512 | tf_op jit(solution)/shard_map/dot_general | solution.py:71
  9.6 2.4 %collective-permute-start = (bf16[3,1536]{1,0:T(4,128)(2,1)S(1)}, bf16[3,1536]{1,0:T(4,128)(2,1)S(1)}, u32[]{:S(2)}, u32[]{:S(2)}) collective-permute-start(bf16[3,1536]{1,0:T(4,128)(2,1)S(1)} %slice.49), channel_id=1, source_target_pairs={{0,1},{1,2},{2,3},{3,4},{4,5},{5,6},{6,7},{7,8},{8,9},{9,10},{10,1... | collective-permute-start | bytes 27656 | tf_op jit(solution)/shard_map/ppermute | solution.py:18
  12.1 0.7 collective-permute-done
  13.1 0.7 fusion.8
  13.7 0.3 multiply_convert_fusion.1
  14.3 0.9 fusion.40
  15.3 0.7 all-gather.5.cloned.1.call-update
  16.1 0.7 all-gather.7.cloned.1.call-update
  17.0 80.1 %all-gather.9.cloned.1.call-done = f32[256,64,64]{2,1,0:T(8,128)} async-done(((f32[8,64,64]{2,1,0:T(8,128)}), f32[256,64,64]{2,1,0:T(8,128)}) %all-gather.9.cloned.1.call-update) | async-done | bytes 4194320 | tf_op jit(solution)/shard_map/all_gather | solution.py:23
  97.0 34.4 %while.18 = (s32[]{:T(128)}, f32[8,64,64]{2,1,0:T(8,128)S(1)}, s32[]{:T(128)}, f32[32,8,64,64]{3,2,1,0:T(8,128)}, s32[]{:T(128)}, /*index=5*/s32[]{:T(128)}) while((s32[]{:T(128)}, f32[8,64,64]{2,1,0:T(8,128)S(1)}, s32[]{:T(128)}, f32[32,8,64,64]{3,2,1,0:T(8,128)}, s32[]{:T(128)}, /*index=5*/s32[]{:T(128)}) %tuple.49), condition=%wide.region_2.3_spmd.clone, body=%wide.region_1.2_spmd.clone.sunk | while | flops 98308 | bytes 393309 | solution.py:31
  97.0 1.0 add_select_fusion.2
  98.1 1.0 add_select_fusion.2
  99.2 1.0 add_select_fusion.2
  100.2 1.0 add_select_fusion.2
  101.3 1.0 add_select_fusion.2
  102.4 1.1 add_select_fusion.2
  103.5 1.1 add_select_fusion.2
  104.6 1.1 add_select_fusion.2
  105.7 1.0 add_select_fusion.2
  106.8 1.0 add_select_fusion.2
  107.9 1.0 add_select_fusion.2
  108.9 1.0 add_select_fusion.2
  110.0 1.0 add_select_fusion.2
  111.1 1.0 add_select_fusion.2
  112.1 1.0 add_select_fusion.2
  113.2 1.0 add_select_fusion.2
  114.3 1.0 add_select_fusion.2
  115.3 1.0 add_select_fusion.2
  116.4 1.0 add_select_fusion.2
  117.5 1.0 add_select_fusion.2
  118.6 1.0 add_select_fusion.2
  119.6 1.0 add_select_fusion.2
  120.7 1.0 add_select_fusion.2
  121.8 1.0 add_select_fusion.2
  122.8 1.0 add_select_fusion.2
  123.9 1.0 add_select_fusion.2
  125.0 1.0 add_select_fusion.2
  126.1 1.0 add_select_fusion.2
  127.1 1.1 add_select_fusion.2
  128.2 1.1 add_select_fusion.2
  129.3 1.1 add_select_fusion.2
  130.4 1.0 add_select_fusion.2
  131.5 1.1 fusion.33
  132.5 1.8 %multiply_reduce_fusion.1 = (f32[256,8]{0,1:T(8,128)S(1)}, f32[256,8,64]{0,2,1:T(8,128)S(1)}) fusion(f32[8,64,256]{2,1,0:T(8,128)} %fusion.33, bf16[256,8,64]{0,2,1:T(8,128)(2,1)S(1)} %bitcast.28, bf16[256,8,64]{0,2,1:T(8,128)(2,1)S(1)} %bitcast.30, bf16[256,8,64]{0,2,1:T(8,128)(2,1)S(1)} %bitcast.26, pred[256,256]{1,0:T(8,128)(4,1)S(1)} %iota_compare_fusion), kind=kOutput, calls=%fused_computation.41 | convolution fusion | flops 135657472 | bytes 1908736 | tf_op jit(solution)/shard_map/while/body/eval_jaxpr/hts,shd->thd/dot_general | solution.py:49
  134.6 1.5 multiply_reduce_fusion
  136.1 7.9 %all-gather.7.cloned.1.call-done = bf16[2048,512]{1,0:T(8,128)(2,1)} async-done(((bf16[512,512]{1,0:T(8,128)(2,1)}), bf16[2048,512]{1,0:T(8,128)(2,1)}) %all-gather.7.cloned.1.call-update) | async-done | bytes 2097168 | tf_op jit(solution)/shard_map/all_gather | solution.py:117
  144.0 4.5 %fusion.14 = bf16[256,512]{1,0:T(8,128)(2,1)} fusion(f32[256,512]{1,0:T(8,128)S(1)} %get-tuple-element.135, bf16[2048,512]{1,0:T(8,128)(2,1)} %all-gather.7.cloned.1.call-done, bf16[512,2048]{1,0:T(8,128)(2,1)} %all-gather.5.cloned.1.call-done, f32[512]{0:T(512)S(1)} %copy-done.4, f32[256]{0:T(256)S(1)} %add_rsqrt_fusion.1), kind=kOutput, calls=%fused_computation.24 | convolution fusion | flops 1079115776 | bytes 4983808 | tf_op jit(solution)/shard_map/dot_general | solution.py:115
  (29 shorter events, 1.4 us)
Async XLA Ops:
  6.5 1.5 copy-start
  6.5 5.5 %copy-start.2 = (f32[4,1536]{1,0:T(4,128)S(1)}, f32[4,1536]{1,0:T(4,128)}, u32[]{:S(2)}) copy-start(f32[4,1536]{1,0:T(4,128)} %param.14) | copy-start | bytes 73732
  6.5 90.5 %all-gather.9.cloned.1.call-start = ((), (), s32[]{:S(2)}) async-start(), calls=%async_computation.2 | async-start | bytes 8650752 | tf_op jit(solution)/shard_map/all_gather | solution.py:23
  9.6 3.2 %collective-permute-start = (bf16[3,1536]{1,0:T(4,128)(2,1)S(1)}, bf16[3,1536]{1,0:T(4,128)(2,1)S(1)}, u32[]{:S(2)}, u32[]{:S(2)}) collective-permute-start(bf16[3,1536]{1,0:T(4,128)(2,1)S(1)} %slice.49), channel_id=1, source_target_pairs={{0,1},{1,2},{2,3},{3,4},{4,5},{5,6},{6,7},{7,8},{8,9},{9,10},{10,1... | collective-permute-start | bytes 27656 | tf_op jit(solution)/shard_map/ppermute | solution.py:18
  15.3 120.8 %all-gather.5.cloned.1.call-start = ((), (), s32[]{:S(2)}) async-start(), calls=%async_computation | async-start | bytes 2621440 | tf_op jit(solution)/shard_map/all_gather | solution.py:111
  16.0 127.9 %all-gather.7.cloned.1.call-start = ((), (), s32[]{:S(2)}) async-start(), calls=%async_computation.1 | async-start | bytes 2621440 | tf_op jit(solution)/shard_map/all_gather | solution.py:117
  131.4 3.0 %copy-start.3 = (f32[512]{0:T(512)S(1)}, f32[512]{0:T(512)}, u32[]{:S(2)}) copy-start(f32[512]{0:T(512)} %param.16) | copy-start | bytes 6148
  132.5 2.1 %copy-start.1 = (bf16[256,512]{1,0:T(8,128)(2,1)S(1)}, bf16[256,512]{1,0:T(8,128)(2,1)}, u32[]{:S(2)}) copy-start(bf16[256,512]{1,0:T(8,128)(2,1)} %param.11) | copy-start | bytes 786436
  134.4 9.6 %copy-start.4 = (f32[512]{0:T(512)S(1)}, f32[512]{0:T(512)}, u32[]{:S(2)}) copy-start(f32[512]{0:T(512)} %param.17) | copy-start | bytes 6148
Sparse Core Ops, SparseCore 0:
  15.4 81.5 all-gather.8
  98.6 21.1 all-gather.4
  121.4 22.5 all-gather.6
where the time goes:
time: 156 us; the launch traced here: 155 us
  waiting for transfers between devices  90.1 us (58%)
  other arithmetic  36.2 us (23%)
  between operations  13.3 us (9%)
  matrix products  11.4 us (7%)
  starting transfers between devices  2.48 us (2%)
    all_gather x1, waiting for transfers between devices, prefix_2(): everything = lax.all_gather(x, axis)  80.1 us
    select_n x32, other arithmetic, turn(): return jnp.where(reached, new, before)  33.6 us
    all_gather x1, waiting for transfers between devices, body(): lax.all_gather(down_weight, 'seq', axis=0, tiled=True)  7.88 us
    dot_general x1, matrix products, body(): jnp.dot(inner_act, lax.all_gather(down_weight, 'seq', axis=0, tiled=True)...  4.54 us
  transfers between devices with their start and end apart: 4, of which 3 were waited for; matrix products, arithmetic and copies ran while one was open for 25% of the time, Pallas kernels for 0%

commit v1 on v0

v1 whole, which is shorter than its diff:
```python
import functools

import jax
import jax.numpy as jnp
from jax import lax
from jax.experimental import pallas as pl
from jax.experimental.pallas import tpu as pltpu
from jax.sharding import PartitionSpec as P

HEADS = 8
HEAD = 64
KERNEL = 4
BLOCK = 256
EPSILON = 1e-05
AXES = ("grp", "seq")
LAG = 8
F32 = jnp.float32
BF16 = jnp.bfloat16


def vmem():
    return pl.BlockSpec(memory_space=pltpu.VMEM)


def dot(a, b):
    return jnp.dot(a, b, preferred_element_type=F32)


def rms_rows(values, gain):
    mean_square = jnp.mean(values * values, axis=-1, keepdims=True)
    return values * lax.rsqrt(mean_square + EPSILON) * gain


def project_kernel(frames_ref, gain_ref, weight_ref, out_ref, tail_ref):
    rows = frames_ref.shape[0]
    normed = rms_rows(frames_ref[...].astype(F32), gain_ref[...]).astype(BF16)
    projected = dot(normed, weight_ref[...]).astype(BF16)
    out_ref[...] = projected
    tail_ref[...] = projected[rows - 2 * LAG :].astype(F32)[LAG:].astype(BF16)


def lanes(shape, dim):
    return lax.broadcasted_iota(jnp.int32, shape, dim)


def convolve_kernel(
    projected_ref, before_ref, taps_ref, q_ref, k_ref, v_ref, state_ref, extended
):
    rows, channels = projected_ref.shape
    width = channels // 3
    extended[:LAG, :] = before_ref[...].astype(F32)
    extended[LAG:, :] = projected_ref[...].astype(F32)
    for part, ref in enumerate((q_ref, k_ref, v_ref)):
        at = slice(part * width, (part + 1) * width)
        total = jnp.zeros((rows, width), F32)
        for offset in range(KERNEL):
            total = total + taps_ref[offset : offset + 1, at] * extended[LAG - offset : LAG - offset + rows, at]
        if part < 2:
            total = total / (1.0 + jnp.exp(-total))
        ref[...] = total.astype(BF16)
    half = width // 2
    folded = []
    same = lanes((half, half), 0) // HEAD == lanes((half, half), 1) // HEAD
    for g in range(2):
        at = slice(g * half, (g + 1) * half)
        outer = lax.dot_general(
            k_ref[:, at], v_ref[:, at], (((0,), (0,)), ((), ())), preferred_element_type=F32
        )
        outer = jnp.where(same, outer, 0.0)
        fold = outer[:, : 2 * HEAD]
        for start in range(2 * HEAD, half, 2 * HEAD):
            fold = fold + outer[:, start : start + 2 * HEAD]
        folded.append(fold + pltpu.roll(fold, HEAD, 1))
    low = lanes(folded[0].shape, 1) < HEAD
    state_ref[...] = jnp.where(low, folded[0], folded[1])


def local_kernel(q_ref, k_ref, v_ref, out_ref):
    rows = q_ref.shape[0]
    causal = lanes((rows, rows), 0) >= lanes((rows, rows), 1)
    pair = 2 * HEAD
    first = lanes((rows, pair), 1) < HEAD
    for p in range(HEADS // 2):
        at = slice(p * pair, (p + 1) * pair)
        q, k, v = q_ref[:, at], k_ref[:, at], v_ref[:, at]
        total = None
        for side in range(2):
            mine = first if side == 0 else jnp.logical_not(first)
            zero = jnp.zeros_like(k)
            scores = lax.dot_general(
                q, jnp.where(mine, k, zero), (((1,), (1,)), ((), ())), preferred_element_type=F32
            )
            scores = jnp.where(causal, scores, 0.0).astype(BF16)
            part = dot(scores, jnp.where(mine, v, zero))
            total = part if total is None else total + part
        out_ref[:, at] = total


def gelu(x):
    return 0.5 * x * (1.0 + jnp.tanh(0.7978845608028654 * (x + 0.044715 * (x * x * x))))


def tail_kernel(count, *refs):
    (q_ref, local_ref, state_ref, frames_ref, head_gain_ref, ffn_gain_ref, out_w_ref) = refs[:7]
    ups, downs = refs[7 : 7 + count], refs[7 + count : 7 + 2 * count]
    out_ref = refs[7 + 2 * count]
    up_buf, down_buf, up_sem, down_sem = refs[8 + 2 * count :]
    copies = []
    for i in range(count):
        a = pltpu.make_async_copy(ups[i], up_buf.at[i], up_sem.at[i])
        b = pltpu.make_async_copy(downs[i], down_buf.at[i], down_sem.at[i])
        a.start()
        b.start()
        copies.append((a, b))
    width = q_ref.shape[1]
    half = width // 2
    state = state_ref[...]
    turned = pltpu.roll(state, HEAD, 1)
    low = lanes(state.shape, 1) < HEAD
    same = lanes((half, half), 0) // HEAD == lanes((half, half), 1) // HEAD
    mean_of = jnp.where(same, 1.0 / HEAD, 0.0).astype(BF16)
    headed = []
    for g in range(2):
        at = slice(g * half, (g + 1) * half)
        both = jnp.where(low, state, turned) if g == 0 else jnp.where(low, turned, state)
        spread = jnp.concatenate([both] * (half // (2 * HEAD)), axis=1)
        spread = jnp.where(same, spread, 0.0).astype(BF16)
        attended = local_ref[:, at] + dot(q_ref[:, at], spread)
        square = attended * attended
        upper = square.astype(BF16)
        lower = (square - upper.astype(F32)).astype(BF16)
        mean = dot(upper, mean_of) + dot(lower, mean_of)
        headed.append(
            (attended * lax.rsqrt(mean + EPSILON) * head_gain_ref[:, at]).astype(BF16)
        )
    residual = frames_ref[...].astype(F32) + dot(jnp.concatenate(headed, axis=1), out_w_ref[...])
    normed = rms_rows(residual, ffn_gain_ref[...]).astype(BF16)
    total = residual
    for i in range(count):
        copies[i][0].wait()
        inner = gelu(dot(normed, up_buf[i])).astype(BF16)
        copies[i][1].wait()
        total = total + dot(inner, down_buf[i])
    out_ref[...] = total.astype(BF16)


def shapes(*pairs):
    return tuple(jax.ShapeDtypeStruct(s, d) for s, d in pairs)


def swap(value, bit, count):
    return lax.ppermute(value, AXES, [(i, i ^ bit) for i in range(count)])


def body(
    devices,
    seqs,
    frames_in,
    norm_gain,
    qkv_weight,
    conv_weight,
    out_weight,
    head_gain,
    ffn_gain,
    up_weight,
    down_weight,
):
    rows, width = frames_in.shape
    place = lax.axis_index(AXES)
    projected, tail = pl.pallas_call(
        project_kernel,
        out_shape=shapes(((rows, 3 * width), BF16), ((LAG, 3 * width), BF16)),
        in_specs=[vmem()] * 3,
        out_specs=(vmem(), vmem()),
        name="project",
    )(frames_in, norm_gain.reshape(1, -1), qkv_weight)
    before = lax.ppermute(tail, AXES, [(i, i + 1) for i in range(devices - 1)])
    queries, key_rows, value_rows, state = pl.pallas_call(
        convolve_kernel,
        out_shape=shapes(*[((rows, width), BF16)] * 3, ((width // 2, 2 * HEAD), F32)),
        in_specs=[vmem()] * 3,
        out_specs=(vmem(),) * 4,
        scratch_shapes=[pltpu.VMEM((LAG + rows, 3 * width), F32)],
        name="convolve",
    )(projected, before, conv_weight)

    own = (up_weight, down_weight)
    total, prefix = state, jnp.zeros_like(state)
    bit = 1
    while bit < devices:
        came = swap(total.astype(BF16), bit, devices).astype(F32)
        prefix = prefix + jnp.where((place & bit) != 0, came, 0.0)
        total = total + came
        if bit == seqs // 2:
            own, total = lax.optimization_barrier((own, total))
        bit *= 2

    local = pl.pallas_call(
        local_kernel,
        out_shape=jax.ShapeDtypeStruct((rows, width), F32),
        in_specs=[vmem()] * 3,
        out_specs=vmem(),
        name="local",
    )(queries, key_rows, value_rows)

    sets = [own]
    bit = 2
    while bit < seqs:
        sets = sets + [tuple(swap(w, bit, devices) for w in s) for s in sets]
        bit *= 2
    if seqs > 1:
        sets = [
            t
            for s in sets
            for t in (s, tuple(swap(w, 1, devices) for w in s))
        ]
    count = len(sets)
    hidden = up_weight.shape[1]
    anywhere = pl.BlockSpec(memory_space=pl.ANY)
    return pl.pallas_call(
        functools.partial(tail_kernel, count),
        out_shape=jax.ShapeDtypeStruct((rows, width), BF16),
        in_specs=[vmem()] * 7 + [anywhere] * (2 * count),
        out_specs=vmem(),
        scratch_shapes=[
            pltpu.VMEM((count, width, hidden), BF16),
            pltpu.VMEM((count, hidden, width), BF16),
            pltpu.SemaphoreType.DMA((count,)),
            pltpu.SemaphoreType.DMA((count,)),
        ],
        name="tail",
    )(
        queries,
        local,
        prefix,
        frames_in,
        head_gain.reshape(1, -1),
        ffn_gain.reshape(1, -1),
        out_weight,
        *[s[0] for s in sets],
        *[s[1] for s in sets],
    )


def solution(mesh):
    sizes = dict(mesh.shape)
    in_specs = (
        P(AXES, None),
        P(),
        P(),
        P(),
        P(),
        P(),
        P(),
        P(None, "seq"),
        P("seq", None),
    )
    return jax.shard_map(
        functools.partial(body, sizes["grp"] * sizes["seq"], sizes["seq"]),
        mesh=mesh,
        in_specs=in_specs,
        out_specs=P(AXES, None),
        check_vma=False,
    )
```

time: 156 us -> 62.7 us (0.40)
  waiting for transfers between devices: 90.1 us -> 21.8 us
  other arithmetic: 36.2 us -> 3.53 us
  starting transfers between devices: 2.48 us -> 20.4 us
  Pallas kernels: 0 us -> 15 us
  between operations: 13.3 us -> 0.1 us
  matrix products: 11.4 us -> 0 us
    all_gather x3 -> x0, waiting for transfers between devices: 88 us -> none  [the longest x1 80.1 us: prefix_2(): everything = lax.all_gather(x, axis)]
    select_n x32 -> x0, other arithmetic: 33.6 us -> none  [turn(): return jnp.where(reached, new, before)]
    ppermute x1 -> x12, waiting for transfers between devices: 0.73 us -> 21.8 us  [the longest x11 20.8 us: swap(): return lax.ppermute(value, AXES, [(i, i ^ bit) for i in range(count)])]
    ppermute x1 -> x12, starting transfers between devices: 2.4 us -> 20.4 us  [the longest x11 18 us: swap(): return lax.ppermute(value, AXES, [(i, i ^ bit) for i in range(count)])]
    pallas_call x0 -> x4, Pallas kernels: none -> 15 us  [the longest x1 5.73 us: body(): pl.pallas_call(functools.partial(tail_kernel, count), out_shape=jax.Shape...]
    dot_general x6 -> x0, matrix products: 11.4 us -> none  [the longest x1 4.54 us: body(): jnp.dot(inner_act, lax.all_gather(down_weight, 'seq', axis=0, tiled=True)...]
  transfers between devices with their start and end apart: 4 -> 12, of which waited for: 3 -> 7; matrix products, arithmetic and copies ran while one was open for 25% -> 1% of each run, Pallas kernels for 0% -> 5%
where the time goes in v1:
time: 62.7 us; the launch traced here: 62.4 us
  waiting for transfers between devices  21.8 us (35%)
  starting transfers between devices  20.4 us (33%)
  Pallas kernels  15 us (24%)
  other arithmetic  3.53 us (6%)
  local copies, waits for them, and re-layouts  1.54 us (2%)
    ppermute x11, waiting for transfers between devices, swap(): return lax.ppermute(value, AXES, [(i, i ^ bit) for i in range(count)])  20.8 us
    ppermute x11, starting transfers between devices, swap(): return lax.ppermute(value, AXES, [(i, i ^ bit) for i in range(count)])  18 us
    pallas_call x1, Pallas kernels, body(): pl.pallas_call(functools.partial(tail_kernel, count), out_shape=jax.Shape...  5.73 us
    pallas_call x1, Pallas kernels, body(): pl.pallas_call(convolve_kernel, out_shape=shapes(*[((rows, width), BF16)]...  3.25 us
    pallas_call x1, Pallas kernels, body(): pl.pallas_call(project_kernel, out_shape=shapes(((rows, 3 * width), BF16)...  3.11 us
    pallas_call x1, Pallas kernels, body(): pl.pallas_call(local_kernel, out_shape=jax.ShapeDtypeStruct((rows, width)...  2.92 us
    ppermute x1, starting transfers between devices, body(): before = lax.ppermute(tail, AXES, [(i, i + 1) for i in range(devices - 1)])  2.39 us
    convert_element_type x5, other arithmetic, body(): came = swap(total.astype(BF16), bit, devices).astype(F32)  1.9 us
  transfers between devices with their start and end apart: 12, of which 7 were waited for; matrix products, arithmetic and copies ran while one was open for 1% of the time, Pallas kernels for 5%

profile of v1, /device:TPU:0, one launch (start us, length us, event | category | flops | bytes accessed | tf_op | source)
XLA Modules:
  0.0 62.4 jit_solution(17581875225300648547)
XLA Ops:
  0.0 0.0 copy-start
  0.0 0.0 copy-start.1
  0.0 3.1 %project.1 = (bf16[256,1536]{1,0:T(8,128)(2,1)}, bf16[8,1536]{1,0:T(8,128)(2,1)}) custom-call(bf16[256,512]{1,0:T(8,128)(2,1)} %refs_3_.1, f32[1,512]{1,0:T(1,128)} %bitcast.5, bf16[512,1536]{1,0:T(8,128)(2,1)} %weight_ref.1), custom_call_target="tpu_custom_call" | custom-call | tf_op jit(solution)/shard_map/project/pallas_call | solution.py:170
  3.1 2.4 %collective-permute-start = (bf16[8,1536]{1,0:T(8,128)(2,1)}, bf16[8,1536]{1,0:T(8,128)(2,1)S(1)}, u32[]{:S(2)}, u32[]{:S(2)}) collective-permute-start(bf16[8,1536]{1,0:T(8,128)(2,1)} %get-tuple-element.15), channel_id=1, source_target_pairs={{0,1},{1,2},{2,3},{3,4},{4,5},{5,6},{6,7},{7,8},{8,9},{9,10},{10,1... | collective-permute-start | bytes 73736 | tf_op jit(solution)/shard_map/ppermute | solution.py:177
  5.5 1.0 %collective-permute-done.before_ref = bf16[8,1536]{1,0:T(8,128)(2,1)S(1)} collective-permute-done((bf16[8,1536]{1,0:T(8,128)(2,1)}, bf16[8,1536]{1,0:T(8,128)(2,1)S(1)}, u32[]{:S(2)}, u32[]{:S(2)}) %collective-permute-start) | collective-permute-done | bytes 24608 | tf_op jit(solution)/shard_map/ppermute | solution.py:177
  6.6 0.0 copy-start.6
  6.6 0.6 copy-done.6
  7.2 3.3 %convolve.1 = (bf16[256,512]{1,0:T(8,128)(2,1)}, bf16[256,512]{1,0:T(8,128)(2,1)}, bf16[256,512]{1,0:T(8,128)(2,1)}, f32[256,128]{1,0:T(8,128)}) custom-call(bf16[256,1536]{1,0:T(8,128)(2,1)} %get-tuple-element.14.projected_ref, bf16[8,1536]{1,0:T(8,128)(2,1)} %copy-done.6, f32[4,1536]{1,0:T(4,128)} %taps_ref.1), custom_call_target="tpu_custom_call" | custom-call | tf_op jit(solution)/shard_map/convolve/pallas_call | solution.py:178
  10.4 0.9 %convert_element_type.30 = bf16[256,128]{1,0:T(8,128)(2,1)S(1)} convert(f32[256,128]{1,0:T(8,128)} %get-tuple-element.19) | non-fusion elementwise | flops 32768 | bytes 196608 | tf_op jit(solution)/shard_map/convert_element_type | solution.py:191
  11.3 2.7 %collective-permute-start.1 = (bf16[256,128]{1,0:T(8,128)(2,1)S(1)}, bf16[256,128]{1,0:T(8,128)(2,1)S(1)}, u32[]{:S(2)}, u32[]{:S(2)}) collective-permute-start(bf16[256,128]{1,0:T(8,128)(2,1)S(1)} %convert_element_type.30), channel_id=1, source_target_pairs={{0,1},{1,0},{2,3},{3,2},{4,5},{5,4},{6,7},{7,6},{8,9},{9,8},{10,11... | collective-permute-start | bytes 196616 | tf_op jit(solution)/shard_map/ppermute | solution.py:152
  14.0 0.9 %collective-permute-done.1 = bf16[256,128]{1,0:T(8,128)(2,1)S(1)} collective-permute-done((bf16[256,128]{1,0:T(8,128)(2,1)S(1)}, bf16[256,128]{1,0:T(8,128)(2,1)S(1)}, u32[]{:S(2)}, u32[]{:S(2)}) %collective-permute-start.1) | collective-permute-done | bytes 65568 | tf_op jit(solution)/shard_map/ppermute | solution.py:152
  14.9 0.9 %fusion.5 = bf16[256,128]{1,0:T(8,128)(2,1)S(1)} fusion(f32[256,128]{1,0:T(8,128)} %get-tuple-element.19, bf16[256,128]{1,0:T(8,128)(2,1)S(1)} %collective-permute-done.1), kind=kLoop, calls=%fused_computation.13 | loop fusion | flops 98304 | bytes 262144 | tf_op jit(solution)/shard_map/convert_element_type | solution.py:191
  15.9 2.6 %collective-permute-start.2 = (bf16[256,128]{1,0:T(8,128)(2,1)S(1)}, bf16[256,128]{1,0:T(8,128)(2,1)S(1)}, u32[]{:S(2)}, u32[]{:S(2)}) collective-permute-start(bf16[256,128]{1,0:T(8,128)(2,1)S(1)} %fusion.5), channel_id=1, source_target_pairs={{0,2},{1,3},{2,0},{3,1},{4,6},{5,7},{6,4},{7,5},{8,10},{9,11},{10,... | collective-permute-start | bytes 196616 | tf_op jit(solution)/shard_map/ppermute | solution.py:152
  18.5 2.4 %collective-permute-done.2 = bf16[256,128]{1,0:T(8,128)(2,1)S(1)} collective-permute-done((bf16[256,128]{1,0:T(8,128)(2,1)S(1)}, bf16[256,128]{1,0:T(8,128)(2,1)S(1)}, u32[]{:S(2)}, u32[]{:S(2)}) %collective-permute-start.2) | collective-permute-done | bytes 65568 | tf_op jit(solution)/shard_map/ppermute | solution.py:152
  20.9 0.9 %convert_add_fusion.2 = f32[256,128]{1,0:T(8,128)S(1)} fusion(bf16[256,128]{1,0:T(8,128)(2,1)S(1)} %collective-permute-done.2, f32[256,128]{1,0:T(8,128)} %get-tuple-element.19, bf16[256,128]{1,0:T(8,128)(2,1)S(1)} %collective-permute-done.1), kind=kLoop, calls=%fused_computation.4 | loop fusion | flops 131072 | bytes 393216 | tf_op jit(solution)/shard_map/add | solution.py:193
  21.8 0.0 copy-done
  21.8 1.9 %collective-permute-start.7 = (bf16[512,512]{1,0:T(8,128)(2,1)S(1)}, bf16[512,512]{1,0:T(8,128)(2,1)S(1)}, u32[]{:S(2)}, u32[]{:S(2)}) collective-permute-start(bf16[512,512]{1,0:T(8,128)(2,1)S(1)} %copy-done), channel_id=1, source_target_pairs={{0,2},{1,3},{2,0},{3,1},{4,6},{5,7},{6,4},{7,5},{8,10},{9,11},{10,... | collective-permute-start | bytes 1572872 | tf_op jit(solution)/shard_map/ppermute | solution.py:152
  23.7 0.0 copy-done.1
  23.8 0.2 collective-permute-start.10
  23.9 2.8 %collective-permute-start.3 = (bf16[256,128]{1,0:T(8,128)(2,1)S(1)}, bf16[256,128]{1,0:T(8,128)(2,1)S(1)}, u32[]{:S(2)}, u32[]{:S(2)}) collective-permute-start(bf16[256,128]{1,0:T(8,128)(2,1)S(1)} %convert_element_type.34), channel_id=1, source_target_pairs={{0,4},{1,5},{2,6},{3,7},{4,0},{5,1},{6,2},{7,3},{8,12},{9,13},{10,... | collective-permute-start | bytes 196616 | tf_op jit(solution)/shard_map/ppermute | solution.py:152
  26.7 2.2 %collective-permute-done.3 = bf16[256,128]{1,0:T(8,128)(2,1)S(1)} collective-permute-done((bf16[256,128]{1,0:T(8,128)(2,1)S(1)}, bf16[256,128]{1,0:T(8,128)(2,1)S(1)}, u32[]{:S(2)}, u32[]{:S(2)}) %collective-permute-start.3) | collective-permute-done | bytes 65568 | tf_op jit(solution)/shard_map/ppermute | solution.py:152
  29.0 3.1 %collective-permute-start.4 = (bf16[256,128]{1,0:T(8,128)(2,1)S(1)}, bf16[256,128]{1,0:T(8,128)(2,1)S(1)}, u32[]{:S(2)}, u32[]{:S(2)}) collective-permute-start(bf16[256,128]{1,0:T(8,128)(2,1)S(1)} %fusion.6), channel_id=1, source_target_pairs={{0,8},{1,9},{2,10},{3,11},{4,12},{5,13},{6,14},{7,15},{8,0},{9,1},... | collective-permute-start | bytes 196616 | tf_op jit(solution)/shard_map/ppermute | solution.py:152
  32.1 0.0 collective-permute-start.6
  32.1 0.5 collective-permute-start.9
  32.6 4.1 %collective-permute-done.7.refs_9_ = bf16[512,512]{1,0:T(8,128)(2,1)S(1)} collective-permute-done((bf16[512,512]{1,0:T(8,128)(2,1)S(1)}, bf16[512,512]{1,0:T(8,128)(2,1)S(1)}, u32[]{:S(2)}, u32[]{:S(2)}) %collective-permute-start.7) | collective-permute-done | bytes 524320 | tf_op jit(solution)/shard_map/ppermute | solution.py:152
  36.7 0.0 copy-start.2
  36.7 0.0 collective-permute-start.8
  36.7 9.8 %collective-permute-done.10.refs_13_ = bf16[512,512]{1,0:T(8,128)(2,1)S(1)} collective-permute-done((bf16[512,512]{1,0:T(8,128)(2,1)S(1)}, bf16[512,512]{1,0:T(8,128)(2,1)S(1)}, u32[]{:S(2)}, u32[]{:S(2)}) %collective-permute-start.10) | collective-permute-done | bytes 524320 | tf_op jit(solution)/shard_map/ppermute | solution.py:152
  46.5 0.0 copy-start.3
  46.5 0.0 collective-permute-start.11
  46.5 0.0 collective-permute-done.4
  46.6 4.2 %collective-permute-start.5 = (bf16[256,128]{1,0:T(8,128)(2,1)S(1)}, bf16[256,128]{1,0:T(8,128)(2,1)S(1)}, u32[]{:S(2)}, u32[]{:S(2)}) collective-permute-start(bf16[256,128]{1,0:T(8,128)(2,1)S(1)} %fusion.4), channel_id=1, source_target_pairs={{0,16},{1,17},{2,18},{3,19},{4,20},{5,21},{6,22},{7,23},{8,24},{9,... | collective-permute-start | bytes 196616 | tf_op jit(solution)/shard_map/ppermute | solution.py:152
  50.8 2.9 %local.1.refs_1_ = f32[256,512]{1,0:T(8,128)} custom-call(bf16[256,512]{1,0:T(8,128)(2,1)} %get-tuple-element.16.q_ref.refs_0_, bf16[256,512]{1,0:T(8,128)(2,1)} %get-tuple-element.17.k_ref, bf16[256,512]{1,0:T(8,128)(2,1)} %get-tuple-element.18.v_ref), custom_call_target="tpu_custom_call" | custom-call | tf_op jit(solution)/shard_map/local/pallas_call | solution.py:198
  53.7 1.2 %collective-permute-done.5 = bf16[256,128]{1,0:T(8,128)(2,1)S(1)} collective-permute-done((bf16[256,128]{1,0:T(8,128)(2,1)S(1)}, bf16[256,128]{1,0:T(8,128)(2,1)S(1)}, u32[]{:S(2)}, u32[]{:S(2)}) %collective-permute-start.5) | collective-permute-done | bytes 65568 | tf_op jit(solution)/shard_map/ppermute | solution.py:152
  55.0 0.7 %fusion.3.refs_2_ = f32[256,128]{1,0:T(8,128)} fusion(bf16[256,128]{1,0:T(8,128)(2,1)S(1)} %collective-permute-done.1, bf16[256,128]{1,0:T(8,128)(2,1)S(1)} %collective-permute-done.2, bf16[256,128]{1,0:T(8,128)(2,1)S(1)} %collective-permute-done.3, bf16[256,128]{1,0:T(8,128)(2,1)S(1)} %collective-permute-done.4, ...), kind=kLoop, calls=%fused_computation.11 | loop fusion | flops 458752 | bytes 458757 | tf_op jit(solution)/shard_map/add | solution.py:192
  55.7 0.0 collective-permute-done.6.refs_8_
  55.7 0.0 copy-start.4
  55.7 0.0 collective-permute-done.9.refs_12_
  55.7 0.0 copy-start.5
  55.7 0.0 collective-permute-done.8.refs_10_
  55.7 0.0 collective-permute-done.11.refs_14_
  55.7 0.0 copy-done.2
  55.7 0.0 copy-done.3
  55.7 0.7 %copy-done.4 = bf16[512,512]{1,0:T(8,128)(2,1)} copy-done((bf16[512,512]{1,0:T(8,128)(2,1)}, bf16[512,512]{1,0:T(8,128)(2,1)S(1)}, u32[]{:S(2)}) %copy-start.4) | copy-done | bytes 524312
  56.5 0.2 copy-done.5
  56.7 5.7 %tail.1 = bf16[256,512]{1,0:T(8,128)(2,1)} custom-call(bf16[256,512]{1,0:T(8,128)(2,1)} %get-tuple-element.16.q_ref.refs_0_, f32[256,512]{1,0:T(8,128)} %local.1.refs_1_, f32[256,128]{1,0:T(8,128)} %fusion.3.refs_2_, bf16[256,512]{1,0:T(8,128)(2,1)} %refs_3_.1, f32[1,512]{1,0:T(1,128)} %bitcast.3, f32[1,512]{1,0:T(1,128)} %bitcast.4, ...), custom_call_target="tpu_custom_call" | custom-call | tf_op jit(solution)/shard_map/tail/pallas_call | solution.py:220
  (3 shorter events, 0.1 us)
Async XLA Ops:
  0.0 21.8 %copy-start = (bf16[512,512]{1,0:T(8,128)(2,1)S(1)}, bf16[512,512]{1,0:T(8,128)(2,1)}, u32[]{:S(2)}) copy-start(bf16[512,512]{1,0:T(8,128)(2,1)} %refs_7_) | copy-start | bytes 1572868
  0.0 23.7 %copy-start.1 = (bf16[512,512]{1,0:T(8,128)(2,1)S(1)}, bf16[512,512]{1,0:T(8,128)(2,1)}, u32[]{:S(2)}) copy-start(bf16[512,512]{1,0:T(8,128)(2,1)} %refs_11_) | copy-start | bytes 1572868
  3.1 3.4 %collective-permute-start = (bf16[8,1536]{1,0:T(8,128)(2,1)}, bf16[8,1536]{1,0:T(8,128)(2,1)S(1)}, u32[]{:S(2)}, u32[]{:S(2)}) collective-permute-start(bf16[8,1536]{1,0:T(8,128)(2,1)} %get-tuple-element.15), channel_id=1, source_target_pairs={{0,1},{1,2},{2,3},{3,4},{4,5},{5,6},{6,7},{7,8},{8,9},{9,10},{10,1... | collective-permute-start | bytes 73736 | tf_op jit(solution)/shard_map/ppermute | solution.py:177
  6.6 0.6 copy-start.6
  11.3 3.6 %collective-permute-start.1 = (bf16[256,128]{1,0:T(8,128)(2,1)S(1)}, bf16[256,128]{1,0:T(8,128)(2,1)S(1)}, u32[]{:S(2)}, u32[]{:S(2)}) collective-permute-start(bf16[256,128]{1,0:T(8,128)(2,1)S(1)} %convert_element_type.30), channel_id=1, source_target_pairs={{0,1},{1,0},{2,3},{3,2},{4,5},{5,4},{6,7},{7,6},{8,9},{9,8},{10,11... | collective-permute-start | bytes 196616 | tf_op jit(solution)/shard_map/ppermute | solution.py:152
  15.9 5.0 %collective-permute-start.2 = (bf16[256,128]{1,0:T(8,128)(2,1)S(1)}, bf16[256,128]{1,0:T(8,128)(2,1)S(1)}, u32[]{:S(2)}, u32[]{:S(2)}) collective-permute-start(bf16[256,128]{1,0:T(8,128)(2,1)S(1)} %fusion.5), channel_id=1, source_target_pairs={{0,2},{1,3},{2,0},{3,1},{4,6},{5,7},{6,4},{7,5},{8,10},{9,11},{10,... | collective-permute-start | bytes 196616 | tf_op jit(solution)/shard_map/ppermute | solution.py:152
  21.8 14.9 %collective-permute-start.7 = (bf16[512,512]{1,0:T(8,128)(2,1)S(1)}, bf16[512,512]{1,0:T(8,128)(2,1)S(1)}, u32[]{:S(2)}, u32[]{:S(2)}) collective-permute-start(bf16[512,512]{1,0:T(8,128)(2,1)S(1)} %copy-done), channel_id=1, source_target_pairs={{0,2},{1,3},{2,0},{3,1},{4,6},{5,7},{6,4},{7,5},{8,10},{9,11},{10,... | collective-permute-start | bytes 1572872 | tf_op jit(solution)/shard_map/ppermute | solution.py:152
  23.8 22.8 %collective-permute-start.10 = (bf16[512,512]{1,0:T(8,128)(2,1)S(1)}, bf16[512,512]{1,0:T(8,128)(2,1)S(1)}, u32[]{:S(2)}, u32[]{:S(2)}) collective-permute-start(bf16[512,512]{1,0:T(8,128)(2,1)S(1)} %copy-done.1), channel_id=1, source_target_pairs={{0,2},{1,3},{2,0},{3,1},{4,6},{5,7},{6,4},{7,5},{8,10},{9,11},{10,... | collective-permute-start | bytes 1572872 | tf_op jit(solution)/shard_map/ppermute | solution.py:152
  23.9 5.0 %collective-permute-start.3 = (bf16[256,128]{1,0:T(8,128)(2,1)S(1)}, bf16[256,128]{1,0:T(8,128)(2,1)S(1)}, u32[]{:S(2)}, u32[]{:S(2)}) collective-permute-start(bf16[256,128]{1,0:T(8,128)(2,1)S(1)} %convert_element_type.34), channel_id=1, source_target_pairs={{0,4},{1,5},{2,6},{3,7},{4,0},{5,1},{6,2},{7,3},{8,12},{9,13},{10,... | collective-permute-start | bytes 196616 | tf_op jit(solution)/shard_map/ppermute | solution.py:152
  29.0 17.6 %collective-permute-start.4 = (bf16[256,128]{1,0:T(8,128)(2,1)S(1)}, bf16[256,128]{1,0:T(8,128)(2,1)S(1)}, u32[]{:S(2)}, u32[]{:S(2)}) collective-permute-start(bf16[256,128]{1,0:T(8,128)(2,1)S(1)} %fusion.6), channel_id=1, source_target_pairs={{0,8},{1,9},{2,10},{3,11},{4,12},{5,13},{6,14},{7,15},{8,0},{9,1},... | collective-permute-start | bytes 196616 | tf_op jit(solution)/shard_map/ppermute | solution.py:152
  32.1 23.6 %collective-permute-start.6 = (bf16[512,512]{1,0:T(8,128)(2,1)S(1)}, bf16[512,512]{1,0:T(8,128)(2,1)S(1)}, u32[]{:S(2)}, u32[]{:S(2)}) collective-permute-start(bf16[512,512]{1,0:T(8,128)(2,1)S(1)} %copy-done), channel_id=1, source_target_pairs={{0,1},{1,0},{2,3},{3,2},{4,5},{5,4},{6,7},{7,6},{8,9},{9,8},{10,11... | collective-permute-start | bytes 1572872 | tf_op jit(solution)/shard_map/ppermute | solution.py:152
  32.1 23.6 %collective-permute-start.9 = (bf16[512,512]{1,0:T(8,128)(2,1)S(1)}, bf16[512,512]{1,0:T(8,128)(2,1)S(1)}, u32[]{:S(2)}, u32[]{:S(2)}) collective-permute-start(bf16[512,512]{1,0:T(8,128)(2,1)S(1)} %copy-done.1), channel_id=1, source_target_pairs={{0,1},{1,0},{2,3},{3,2},{4,5},{5,4},{6,7},{7,6},{8,9},{9,8},{10,11... | collective-permute-start | bytes 1572872 | tf_op jit(solution)/shard_map/ppermute | solution.py:152
  36.7 19.0 %copy-start.2 = (bf16[512,512]{1,0:T(8,128)(2,1)}, bf16[512,512]{1,0:T(8,128)(2,1)S(1)}, u32[]{:S(2)}) copy-start(bf16[512,512]{1,0:T(8,128)(2,1)S(1)} %collective-permute-done.7.refs_9_) | copy-start | bytes 1572868
  36.7 19.0 %collective-permute-start.8 = (bf16[512,512]{1,0:T(8,128)(2,1)S(1)}, bf16[512,512]{1,0:T(8,128)(2,1)}, u32[]{:S(2)}, u32[]{:S(2)}) collective-permute-start(bf16[512,512]{1,0:T(8,128)(2,1)S(1)} %collective-permute-done.7.refs_9_), channel_id=1, source_target_pairs={{0,1},{1,0},{2,3},{3,2},{4,5},{5,4},{6,7},{7,6},{8,9},{9,8},{10,11... | collective-permute-start | bytes 1572872 | tf_op jit(solution)/shard_map/ppermute | solution.py:152
  46.5 9.2 %copy-start.3 = (bf16[512,512]{1,0:T(8,128)(2,1)}, bf16[512,512]{1,0:T(8,128)(2,1)S(1)}, u32[]{:S(2)}) copy-start(bf16[512,512]{1,0:T(8,128)(2,1)S(1)} %collective-permute-done.10.refs_13_) | copy-start | bytes 1572868
  46.5 9.2 %collective-permute-start.11 = (bf16[512,512]{1,0:T(8,128)(2,1)S(1)}, bf16[512,512]{1,0:T(8,128)(2,1)}, u32[]{:S(2)}, u32[]{:S(2)}) collective-permute-start(bf16[512,512]{1,0:T(8,128)(2,1)S(1)} %collective-permute-done.10.refs_13_), channel_id=1, source_target_pairs={{0,1},{1,0},{2,3},{3,2},{4,5},{5,4},{6,7},{7,6},{8,9},{9,8},{10,11... | collective-permute-start | bytes 1572872 | tf_op jit(solution)/shard_map/ppermute | solution.py:152
  46.6 8.4 %collective-permute-start.5 = (bf16[256,128]{1,0:T(8,128)(2,1)S(1)}, bf16[256,128]{1,0:T(8,128)(2,1)S(1)}, u32[]{:S(2)}, u32[]{:S(2)}) collective-permute-start(bf16[256,128]{1,0:T(8,128)(2,1)S(1)} %fusion.4), channel_id=1, source_target_pairs={{0,16},{1,17},{2,18},{3,19},{4,20},{5,21},{6,22},{7,23},{8,24},{9,... | collective-permute-start | bytes 196616 | tf_op jit(solution)/shard_map/ppermute | solution.py:152
  55.7 0.8 %copy-start.4 = (bf16[512,512]{1,0:T(8,128)(2,1)}, bf16[512,512]{1,0:T(8,128)(2,1)S(1)}, u32[]{:S(2)}) copy-start(bf16[512,512]{1,0:T(8,128)(2,1)S(1)} %collective-permute-done.6.refs_8_) | copy-start | bytes 1572868
  55.7 1.0 %copy-start.5 = (bf16[512,512]{1,0:T(8,128)(2,1)}, bf16[512,512]{1,0:T(8,128)(2,1)S(1)}, u32[]{:S(2)}) copy-start(bf16[512,512]{1,0:T(8,128)(2,1)S(1)} %collective-permute-done.9.refs_12_) | copy-start | bytes 1572868
